TPU v7x, 32 devices: a whole 2x2x4 slice. The times are simulated.
32 devices in a mesh: grp: 4 (over x, core), dev: 8 (over z, y).
Axes of the slice: x: 2, y: 2, z: 4, core: 2. Of those that a mesh axis runs over, the one named last changes fastest.
Arguments:
- tables: float32 [4, 65536, 128], P(None, ('grp', 'dev')), may hold values from -6 to 6
- accum: float32 [4, 65536], P(None, ('grp', 'dev')), may hold values from 0.01 to 10
- block_position: int32 [4, 512], replicated, may hold values from 0 to 511, as said below
- lookup_ids: int32 [8192, 4], P(('grp', 'dev')), may hold values from 0 to 65535, as said below
Outputs:
- new_tables: float32 [4, 65536, 128], P('grp', 'dev')
- new_accum: float32 [4, 65536], P('grp', 'dev')
- looked: float32 [8192, 4, 128], P(('grp', 'dev'))
Inputs may be any that keep to these rules, and one draw needn't show every extreme that they name: `block_position`: for each table a permutation of 0 to 511. Old block b lies on the device b // 16 of grp+dev; call its dev index its source, and p // 64 the owner of new block p. For every table, source and owner, at most 9 blocks of that source go to that owner, and 9 is reached. `lookup_ids`: the owner of an id of table t is block_position[t, id // 128] // 64. Among one device's 256 rows, at most 64 ids of one table have one owner, and 64 is reached for every device and table.
All inputs are finite; a program needn't handle non-finite values.
Results may differ from a plain program's by a relative error of at most 0.00002.
Values sent between devices are 32-bit elements; how exact they have to be, the bound alone decides.
A program may use at most 128 MiB of HBM per device.

v0:
```python
import jax
import jax.numpy as jnp
from jax import lax
from jax.sharding import PartitionSpec as P

TILE = 128


def shifted(shard, axis, by):
    peers = lax.axis_size(axis)
    return lax.ppermute(shard, axis, [(i, (i + by) % peers) for i in range(peers)])


def body(tables, accum, block_position, lookup_ids):
    groups = lax.axis_size("grp")
    shards = lax.axis_size("dev")
    my_group = lax.axis_index("grp")
    my_shard = lax.axis_index("dev")
    table_count, old_rows, width = tables.shape
    tile_rows = TILE
    own_rows = lax.dynamic_index_in_dim(tables, my_group, 0, keepdims=False)
    own_sums = lax.dynamic_index_in_dim(accum, my_group, 0, keepdims=False)
    held = jnp.zeros((groups, old_rows, width), jnp.float32)
    held_sums = jnp.zeros((groups, old_rows), jnp.float32)
    held = lax.dynamic_update_index_in_dim(held, own_rows, my_group, 0)
    held_sums = lax.dynamic_update_index_in_dim(held_sums, own_sums, my_group, 0)
    for step_by in range(1, groups):
        wanted = (my_group + step_by) % groups
        send_rows = lax.dynamic_index_in_dim(tables, wanted, 0, keepdims=False)
        send_sums = lax.dynamic_index_in_dim(accum, wanted, 0, keepdims=False)
        got_rows, got_sums = shifted((send_rows, send_sums), "grp", step_by)
        anchor = (my_group - step_by) % groups
        held = lax.dynamic_update_index_in_dim(held, got_rows, anchor, 0)
        held_sums = lax.dynamic_update_index_in_dim(held_sums, got_sums, anchor, 0)
    blocks = held.reshape(groups * old_rows // tile_rows, tile_rows, width)
    block_sums = held_sums.reshape(groups * old_rows // tile_rows, tile_rows)
    local = blocks.shape[0]
    per_old = old_rows // tile_rows
    counter = jnp.arange(local, dtype=jnp.int32)
    old_index = (counter // per_old * shards + my_shard) * per_old + counter % per_old
    position_row = lax.dynamic_index_in_dim(block_position, my_group, 0, keepdims=False)
    new_place = position_row[old_index]
    target = new_place // local
    slot_place = new_place % local
    longer = local // 2 + 1
    capacity = -(-longer // shards) + -(-(local - longer) // shards)
    marks = (target[:, None] == jnp.arange(shards, dtype=jnp.int32)[None, :]).astype(jnp.int32)
    order_in = jnp.sum((jnp.cumsum(marks, axis=0) - marks) * marks, axis=1)
    slot_index = target * capacity + order_in
    source_of = jnp.zeros((shards * capacity,), jnp.int32).at[slot_index].set(counter)
    filled = jnp.zeros((shards * capacity,), jnp.int32).at[slot_index].set(1)
    weight = filled.astype(jnp.float32)
    send_blocks = (blocks[source_of] * weight[:, None, None]).reshape(
        shards, capacity, tile_rows, width
    )
    send_sums = (block_sums[source_of] * weight[:, None]).reshape(shards, capacity, tile_rows)
    send_place = jnp.where(filled == 1, slot_place[source_of], -1).reshape(shards, capacity)
    got_blocks, got_sums, got_place = (
        lax.all_to_all(send_blocks, "dev", split_axis=0, concat_axis=0, tiled=True),
        lax.all_to_all(send_sums, "dev", split_axis=0, concat_axis=0, tiled=True),
        lax.all_to_all(send_place, "dev", split_axis=0, concat_axis=0, tiled=True),
    )
    flat_place = got_place.reshape(-1)
    landing = jnp.where(flat_place >= 0, flat_place, local)
    picker = (
        jnp.zeros((local,), jnp.int32)
        .at[landing]
        .set(jnp.arange(shards * capacity, dtype=jnp.int32), mode="drop")
    )
    new_blocks = got_blocks.reshape(shards * capacity, tile_rows, width)[picker]
    new_sums = got_sums.reshape(shards * capacity, tile_rows)[picker]
    rows_here = local * tile_rows
    new_table = new_blocks.reshape(1, rows_here, width)
    new_accum = new_sums.reshape(1, rows_here)
    look_rows = lookup_ids.shape[0]
    limit = 2 * look_rows // shards
    table_ids = jnp.arange(table_count, dtype=jnp.int32)[None, :]
    id_place = block_position[table_ids, lookup_ids // tile_rows]
    owner = id_place // local
    local_row = id_place % local * tile_rows + lookup_ids % tile_rows
    owner_marks = (owner[..., None] == jnp.arange(shards, dtype=jnp.int32)[None, None, :]).astype(
        jnp.int32
    )
    owner_order = jnp.sum((jnp.cumsum(owner_marks, axis=0) - owner_marks) * owner_marks, axis=2)
    table_grid = jnp.broadcast_to(table_ids, owner.shape)
    asking = (
        jnp.full((table_count, shards, limit), -1, jnp.int32)
        .at[table_grid, owner, owner_order]
        .set(local_row)
    )
    asked = lax.all_to_all(
        lax.all_to_all(asking, "grp", split_axis=0, concat_axis=0, tiled=True),
        "dev",
        split_axis=1,
        concat_axis=1,
        tiled=True,
    )
    wanted_rows = asked.reshape(-1)
    answer = new_blocks.reshape(rows_here, width)[jnp.maximum(wanted_rows, 0)]
    returned = lax.all_to_all(
        lax.all_to_all(
            answer.reshape(groups, shards, limit, width),
            "grp",
            split_axis=0,
            concat_axis=0,
            tiled=True,
        ),
        "dev",
        split_axis=1,
        concat_axis=1,
        tiled=True,
    )
    looked = returned[table_grid, owner, owner_order]
    return (new_table, new_accum, looked)


def solution(mesh):
    placed = (P(None, ("grp", "dev"), None), P(None, ("grp", "dev")), P(), P(("grp", "dev"), None))
    return jax.shard_map(
        body,
        mesh=mesh,
        in_specs=placed,
        out_specs=(P("grp", "dev", None), P("grp", "dev"), P(("grp", "dev"), None, None)),
        check_vma=False,
    )
```

profile of v0, /device:TPU:0, one launch (start us, length us, event | category | flops | bytes accessed | tf_op | source)
XLA Modules:
  0.0 282.3 jit_solution(8048110270913988105)
XLA Ops:
  0.7 2.4 broadcast_in_dim.77
  3.1 1.3 copy-done.1
  4.4 1.2 dynamic-slice_bitcast_fusion
  6.1 2.5 collective-permute-start.1
  8.6 1.5 collective-permute-start.2
  10.4 9.1 %gather_fusion.6 = s32[1024]{0:T(1024)S(1)} fusion(s32[4,512]{1,0:T(4,128)S(1)} %copy-done, s32[1024]{0:T(1024)S(1)} %reshape.390), kind=kCustom, calls=%fused_computation.6 | custom fusion | bytes 16384 | tf_op jit(solution)/shard_map/gather | solution.py:78
  20.1 2.3 reduce-window.6
  23.6 4.3 %scatter_custom_fusion.3 = s32[2048]{0:T(1024)S(1)} fusion(s32[1024]{0:T(1024)S(1)} %reshape.434, s32[1024]{0:T(1024)S(1)} %reshape.436, s32[]{:T(128)} %constant.204.clone.1), kind=kCustom, calls=%fused_computation.76 | custom fusion | bytes 8196
  28.7 3.2 %all-to-all-start.3 = ((s32[4,1,512]{2,1,0:T(1,128)}), s32[4,1,512]{2,1,0:T(1,128)S(1)}, u32[]{:S(2)}, u32[]{:S(2)}) async-start(s32[4,1,512]{2,1,0:T(1,128)} %reshape.470), calls=%async_computation.3 | async-start | bytes 16384 | tf_op jit(solution)/shard_map/all_to_all | solution.py:92
  34.8 1.2 gather_fusion.2
  36.8 17.5 %all-to-all-done.3 = s32[4,1,512]{2,1,0:T(1,128)S(1)} async-done(((s32[4,1,512]{2,1,0:T(1,128)}), s32[4,1,512]{2,1,0:T(1,128)S(1)}, u32[]{:S(2)}, u32[]{:S(2)}) %all-to-all-start.3) | async-done | bytes 8224 | tf_op jit(solution)/shard_map/all_to_all | solution.py:92
  54.3 6.6 %all-to-all-start.1 = ((s32[8,1,9]{2,1,0:T(1,128)}), s32[8,1,9]{2,1,0:T(1,128)S(1)}, u32[]{:S(2)}, u32[]{:S(2)}) async-start(s32[8,1,9]{2,1,0:T(1,128)} %bitcast.14), calls=%async_computation.1 | async-start | bytes 8192 | tf_op jit(solution)/shard_map/all_to_all | solution.py:61
  63.0 2.3 bitcast_dynamic-update-slice_fusion.2
  65.2 2.3 bitcast_dynamic-update-slice_fusion.1
  67.5 2.3 bitcast_dynamic-update-slice_fusion
  69.8 5.2 %gather_fusion.1 = f32[72,128,128]{2,1,0:T(8,128)} fusion(f32[64,128,128]{2,1,0:T(8,128)} %bitcast.6, s32[1024]{0:T(1024)S(1)} %pad_clamp_fusion.1), kind=kCustom, calls=%fused_computation.1 | custom fusion | bytes 9437472 | tf_op jit(solution)/shard_map/gather | solution.py:53
  75.0 6.0 %all-to-all-start.4 = ((s32[8,1,256]{2,1,0:T(1,128)}), s32[8,1,256]{2,1,0:T(1,128)S(1)}, u32[]{:S(2)}, u32[]{:S(2)}) async-start(s32[8,1,256]{2,1,0:T(1,128)} %reshape.472), calls=%async_computation.4 | async-start | bytes 16384 | tf_op jit(solution)/shard_map/all_to_all | solution.py:91
  81.0 4.8 %broadcast_multiply_fusion = f32[8,9,128,128]{3,2,1,0:T(8,128)} fusion(f32[8,9,128,128]{3,2,1,0:T(8,128)} %bitcast.102, f32[8,9]{1,0:T(8,128)S(1)} %mul.73), kind=kLoop, calls=%fused_computation.13 | loop fusion | flops 1179648 | bytes 9437472 | tf_op jit(solution)/shard_map/mul | solution.py:53
  85.8 1.7 all-to-all-done.4
  87.5 4.6 %all-to-all-start = ((f32[8,9,128,128]{3,2,1,0:T(8,128)}), f32[8,9,128,128]{3,2,1,0:T(8,128)}, u32[]{:S(2)}, u32[]{:S(2)}) async-start(f32[8,9,128,128]{3,2,1,0:T(8,128)} %broadcast_multiply_fusion), calls=%async_computation | async-start | bytes 9437184 | tf_op jit(solution)/shard_map/all_to_all | solution.py:59
  95.0 100.2 %all-to-all-done = f32[8,9,128,128]{3,2,1,0:T(8,128)} async-done(((f32[8,9,128,128]{3,2,1,0:T(8,128)}), f32[8,9,128,128]{3,2,1,0:T(8,128)}, u32[]{:S(2)}, u32[]{:S(2)}) %all-to-all-start) | async-done | bytes 4718624 | tf_op jit(solution)/shard_map/all_to_all | solution.py:59
  195.2 5.2 %gather_fusion.3 = f32[64,128,128]{2,1,0:T(8,128)} fusion(f32[72,128,128]{2,1,0:T(8,128)} %bitcast.13, s32[1024]{0:T(1024)S(1)} %pad_clamp_fusion), kind=kCustom, calls=%fused_computation.3 | custom fusion | bytes 8388864 | tf_op jit(solution)/shard_map/gather | solution.py:70
  200.4 9.8 %gather_fusion.7 = f32[2048,128]{1,0:T(8,128)} fusion(f32[8192,128]{1,0:T(8,128)} %bitcast.100, s32[2048]{0:T(1024)S(1)} %broadcast_clamp_fusion), kind=kCustom, calls=%fused_computation.7 | custom fusion | bytes 2105344 | tf_op jit(solution)/shard_map/gather | solution.py:99
  210.2 3.5 %all-to-all-start.5 = ((f32[4,8,64,128]{3,2,1,0:T(8,128)}), f32[4,8,64,128]{3,2,1,0:T(8,128)S(1)}, u32[]{:S(2)}, u32[]{:S(2)}) async-start(f32[4,8,64,128]{3,2,1,0:T(8,128)} %bitcast.30), calls=%async_computation.5 | async-start | bytes 2097152 | tf_op jit(solution)/shard_map/all_to_all | solution.py:101
  214.3 1.6 collective-permute-start.4
  215.9 1.3 collective-permute-start.5
  217.4 10.3 %collective-permute-done.3 = f32[2048]{0:T(1024)S(1)} collective-permute-done((f32[2048]{0:T(1024)S(1)}, f32[2048]{0:T(1024)S(1)}, u32[]{:S(2)}, u32[]{:S(2)}) %collective-permute-start.3) | collective-permute-done | bytes 8224 | tf_op jit(solution)/shard_map/ppermute | solution.py:11
  230.0 3.6 %all-to-all-start.2 = ((f32[8,9,128]{2,1,0:T(8,128)}), f32[8,9,128]{2,1,0:T(8,128)S(1)}, u32[]{:S(2)}, u32[]{:S(2)}) async-start(f32[8,9,128]{2,1,0:T(8,128)} %broadcast_multiply_fusion.1), calls=%async_computation.2 | async-start | bytes 131072 | tf_op jit(solution)/shard_map/all_to_all | solution.py:60
  234.7 5.8 %all-to-all-done.2 = f32[8,9,128]{2,1,0:T(8,128)S(1)} async-done(((f32[8,9,128]{2,1,0:T(8,128)}), f32[8,9,128]{2,1,0:T(8,128)S(1)}, u32[]{:S(2)}, u32[]{:S(2)}) %all-to-all-start.2) | async-done | bytes 36896 | tf_op jit(solution)/shard_map/all_to_all | solution.py:60
  240.5 3.6 %all-to-all-start.6 = ((f32[4,8,64,128]{3,2,0,1:T(8,128)}), f32[4,8,64,128]{3,2,0,1:T(8,128)S(1)}, u32[]{:S(2)}, u32[]{:S(2)}) async-start(f32[4,8,64,128]{3,2,0,1:T(8,128)} %copy.90), calls=%async_computation.6 | async-start | bytes 2097152 | tf_op jit(solution)/shard_map/all_to_all | solution.py:100
  245.5 23.4 %all-to-all-done.6 = f32[4,8,64,128]{3,2,0,1:T(8,128)S(1)} async-done(((f32[4,8,64,128]{3,2,0,1:T(8,128)}), f32[4,8,64,128]{3,2,0,1:T(8,128)S(1)}, u32[]{:S(2)}, u32[]{:S(2)}) %all-to-all-start.6) | async-done | bytes 1048608 | tf_op jit(solution)/shard_map/all_to_all | solution.py:100
  269.0 13.2 %gather_fusion.8 = f32[1024,128]{1,0:T(8,128)} fusion(f32[4,8,64,128]{3,2,1,0:T(8,128)S(1)} %copy.92, s32[1024]{0:T(1024)S(1)} %reshape.404), kind=kCustom, calls=%fused_computation.8 | custom fusion | bytes 1060864 | tf_op jit(solution)/shard_map/gather | solution.py:113
  (98 shorter events, 17.2 us)
Async XLA Ops:
  0.6 9.7 %copy-start = (s32[4,512]{1,0:T(4,128)S(1)}, s32[4,512]{1,0:T(4,128)}, u32[]{:S(2)}) copy-start(s32[4,512]{1,0:T(4,128)} %param.6) | copy-start | bytes 24580
  0.7 3.7 %copy-start.1 = (f32[4,2048,128]{2,1,0:T(8,128)S(1)}, f32[4,2048,128]{2,1,0:T(8,128)}, u32[]{:S(2)}) copy-start(f32[4,2048,128]{2,1,0:T(8,128)} %param.4) | copy-start | bytes 12582916
  4.4 5.7 %copy-start.3 = (s32[256,4]{0,1:T(4,128)S(1)}, s32[256,4]{0,1:T(4,128)}, u32[]{:S(2)}) copy-start(s32[256,4]{0,1:T(4,128)} %param.7) | copy-start | bytes 12292
  5.6 57.3 %collective-permute-start = (f32[2048,128]{1,0:T(8,128)S(1)}, f32[2048,128]{1,0:T(8,128)}, u32[]{:S(2)}, u32[]{:S(2)}) collective-permute-start(f32[2048,128]{1,0:T(8,128)S(1)} %get-tuple-element.6), channel_id=1, source_target_pairs={{0,8},{8,16},{16,24},{24,0},{1,9},{9,17},{17,25},{25,1},{2,10},{10... | collective-permute-start | bytes 3145736 | tf_op jit(solution)/shard_map/ppermute | solution.py:11
  6.1 59.1 %collective-permute-start.1 = (f32[2048,128]{1,0:T(8,128)S(1)}, f32[2048,128]{1,0:T(8,128)}, u32[]{:S(2)}, u32[]{:S(2)}) collective-permute-start(f32[2048,128]{1,0:T(8,128)S(1)} %get-tuple-element.8), channel_id=1, source_target_pairs={{0,16},{8,24},{16,0},{24,8},{1,17},{9,25},{17,1},{25,9},{2,18},{10... | collective-permute-start | bytes 3145736 | tf_op jit(solution)/shard_map/ppermute | solution.py:11
  8.6 58.9 %collective-permute-start.2 = (f32[2048,128]{1,0:T(8,128)S(1)}, f32[2048,128]{1,0:T(8,128)}, u32[]{:S(2)}, u32[]{:S(2)}) collective-permute-start(f32[2048,128]{1,0:T(8,128)S(1)} %get-tuple-element.5), channel_id=1, source_target_pairs={{0,24},{8,0},{16,8},{24,16},{1,25},{9,1},{17,9},{25,17},{2,26},{10... | collective-permute-start | bytes 3145736 | tf_op jit(solution)/shard_map/ppermute | solution.py:11
  10.4 12.5 %copy-start.5 = (s32[3]{0:T(128)S(1)}, s32[3]{0:T(128)}, u32[]{:S(2)}) copy-start(s32[3]{0:T(128)} %constant.221) | copy-start | bytes 40
  10.4 12.6 %copy-start.4 = (s32[3]{0:T(128)S(1)}, s32[3]{0:T(128)}, u32[]{:S(2)}) copy-start(s32[3]{0:T(128)} %constant.224) | copy-start | bytes 40
  28.7 25.6 %all-to-all-start.3 = ((s32[4,1,512]{2,1,0:T(1,128)}), s32[4,1,512]{2,1,0:T(1,128)S(1)}, u32[]{:S(2)}, u32[]{:S(2)}) async-start(s32[4,1,512]{2,1,0:T(1,128)} %reshape.470), calls=%async_computation.3 | async-start | bytes 16384 | tf_op jit(solution)/shard_map/all_to_all | solution.py:92
  54.3 20.6 %all-to-all-start.1 = ((s32[8,1,9]{2,1,0:T(1,128)}), s32[8,1,9]{2,1,0:T(1,128)S(1)}, u32[]{:S(2)}, u32[]{:S(2)}) async-start(s32[8,1,9]{2,1,0:T(1,128)} %bitcast.14), calls=%async_computation.1 | async-start | bytes 8192 | tf_op jit(solution)/shard_map/all_to_all | solution.py:61
  75.0 12.5 %all-to-all-start.4 = ((s32[8,1,256]{2,1,0:T(1,128)}), s32[8,1,256]{2,1,0:T(1,128)S(1)}, u32[]{:S(2)}, u32[]{:S(2)}) async-start(s32[8,1,256]{2,1,0:T(1,128)} %reshape.472), calls=%async_computation.4 | async-start | bytes 16384 | tf_op jit(solution)/shard_map/all_to_all | solution.py:91
  87.5 107.8 %all-to-all-start = ((f32[8,9,128,128]{3,2,1,0:T(8,128)}), f32[8,9,128,128]{3,2,1,0:T(8,128)}, u32[]{:S(2)}, u32[]{:S(2)}) async-start(f32[8,9,128,128]{3,2,1,0:T(8,128)} %broadcast_multiply_fusion), calls=%async_computation | async-start | bytes 9437184 | tf_op jit(solution)/shard_map/all_to_all | solution.py:59
  200.4 13.3 %copy-start.2 = (f32[4,2048]{1,0:T(4,128)S(1)}, f32[4,2048]{1,0:T(4,128)}, u32[]{:S(2)}) copy-start(f32[4,2048]{1,0:T(4,128)} %param.5) | copy-start | bytes 98308
  210.2 19.8 %all-to-all-start.5 = ((f32[4,8,64,128]{3,2,1,0:T(8,128)}), f32[4,8,64,128]{3,2,1,0:T(8,128)S(1)}, u32[]{:S(2)}, u32[]{:S(2)}) async-start(f32[4,8,64,128]{3,2,1,0:T(8,128)} %bitcast.30), calls=%async_computation.5 | async-start | bytes 2097152 | tf_op jit(solution)/shard_map/all_to_all | solution.py:101
  213.8 13.9 %collective-permute-start.3 = (f32[2048]{0:T(1024)S(1)}, f32[2048]{0:T(1024)S(1)}, u32[]{:S(2)}, u32[]{:S(2)}) collective-permute-start(f32[2048]{0:T(1024)S(1)} %bitcast.110), channel_id=1, source_target_pairs={{0,8},{8,16},{16,24},{24,0},{1,9},{9,17},{17,25},{25,1},{2,10},{10... | collective-permute-start | bytes 24584 | tf_op jit(solution)/shard_map/ppermute | solution.py:11
  214.3 14.1 %collective-permute-start.4 = (f32[2048]{0:T(1024)S(1)}, f32[2048]{0:T(1024)S(1)}, u32[]{:S(2)}, u32[]{:S(2)}) collective-permute-start(f32[2048]{0:T(1024)S(1)} %bitcast.109), channel_id=1, source_target_pairs={{0,16},{8,24},{16,0},{24,8},{1,17},{9,25},{17,1},{25,9},{2,18},{10... | collective-permute-start | bytes 24584 | tf_op jit(solution)/shard_map/ppermute | solution.py:11
  215.9 12.6 %collective-permute-start.5 = (f32[2048]{0:T(1024)S(1)}, f32[2048]{0:T(1024)S(1)}, u32[]{:S(2)}, u32[]{:S(2)}) collective-permute-start(f32[2048]{0:T(1024)S(1)} %bitcast.108), channel_id=1, source_target_pairs={{0,24},{8,0},{16,8},{24,16},{1,25},{9,1},{17,9},{25,17},{2,26},{10... | collective-permute-start | bytes 24584 | tf_op jit(solution)/shard_map/ppermute | solution.py:11
  230.0 10.5 %all-to-all-start.2 = ((f32[8,9,128]{2,1,0:T(8,128)}), f32[8,9,128]{2,1,0:T(8,128)S(1)}, u32[]{:S(2)}, u32[]{:S(2)}) async-start(f32[8,9,128]{2,1,0:T(8,128)} %broadcast_multiply_fusion.1), calls=%async_computation.2 | async-start | bytes 131072 | tf_op jit(solution)/shard_map/all_to_all | solution.py:60
  240.5 28.4 %all-to-all-start.6 = ((f32[4,8,64,128]{3,2,0,1:T(8,128)}), f32[4,8,64,128]{3,2,0,1:T(8,128)S(1)}, u32[]{:S(2)}, u32[]{:S(2)}) async-start(f32[4,8,64,128]{3,2,0,1:T(8,128)} %copy.90), calls=%async_computation.6 | async-start | bytes 2097152 | tf_op jit(solution)/shard_map/all_to_all | solution.py:100
where the time goes:
time: 283 us; the launch traced here: 282 us
  waiting for transfers between devices  160 us (57%)
  local copies, waits for them, and re-layouts  71.8 us (25%)
  starting transfers between devices  39.1 us (14%)
  other arithmetic  10.6 us (4%)
    all_to_all x1, waiting for transfers between devices, body(): lax.all_to_all(send_blocks, 'dev', split_axis=0, concat_axis=0, tiled=True)  100 us
    all_to_all x1, waiting for transfers between devices, body(): lax.all_to_all(lax.all_to_all(answer.reshape(groups, shards, limit, width...  23.4 us
    all_to_all x1, waiting for transfers between devices, body(): lax.all_to_all(asking, 'grp', split_axis=0, concat_axis=0, tiled=True)  17.5 us
    gather x1, local copies, waits for them, and re-layouts, body(): looked = returned[table_grid, owner, owner_order]  13.2 us
    ppermute x6, waiting for transfers between devices, shifted(): lax.ppermute(shard, axis, [(i, (i + by) % peers) for i in range(peers)])  10.9 us
    gather x1, local copies, waits for them, and re-layouts, body(): answer = new_blocks.reshape(rows_here, width)[jnp.maximum(wanted_rows, 0)]  9.77 us
    gather x5, local copies, waits for them, and re-layouts, body(): id_place = block_position[table_ids, lookup_ids // tile_rows]  9.55 us
    ppermute x6, starting transfers between devices, shifted(): lax.ppermute(shard, axis, [(i, (i + by) % peers) for i in range(peers)])  7.92 us
  transfers between devices with their start and end apart: 13, of which 7 were waited for; matrix products, arithmetic and copies ran while one was open for 17% of the time, Pallas kernels for 0%

commit v1 on v0

v1 whole, which is shorter than its diff:
```python
import functools

import jax
import jax.numpy as jnp
from jax import lax
from jax.experimental import pallas as pl
from jax.experimental.pallas import tpu as pltpu
from jax.sharding import PartitionSpec as P

TILE = 128
CHUNKS = 4
MESH = pl.DeviceIdType.MESH


def kernel(groups, shards, capacity, limit, *refs):
    source_of, picker, final, tables, sums, asking = refs[:6]
    new_table, new_sums, looked = refs[6:9]
    held = refs[9 : 9 + CHUNKS]
    send = refs[9 + CHUNKS : 9 + 2 * CHUNKS]
    got = refs[9 + 2 * CHUNKS : 9 + 3 * CHUNKS]
    (
        held_sums,
        send_sums,
        got_sums,
        table,
        asked,
        asked_scalar,
        answer,
        returned,
        grp_send,
        grp_recv,
        dev_send,
        dev_recv,
        ask_sem,
        ans_sem,
        own_grp,
        own_dev,
        own_sem,
        out_sem,
    ) = refs[9 + 3 * CHUNKS :]
    my_group = lax.axis_index("grp")
    my_shard = lax.axis_index("dev")
    devices = groups * shards
    me = my_group * shards + my_shard
    per_old = tables.shape[1]
    tile_rows = tables.shape[2]
    piece = tile_rows // CHUNKS
    local = groups * per_old
    slots = shards * capacity

    def coords(peer):
        return (peer // shards, peer % shards)

    def remote(src, dst, send_sem, recv_sem, device):
        return pltpu.make_async_remote_copy(
            src_ref=src,
            dst_ref=dst,
            send_sem=send_sem,
            recv_sem=recv_sem,
            device_id=device,
            device_id_type=MESH,
        )

    barrier = pltpu.get_barrier_semaphore()

    def greet(step, carry):
        pl.semaphore_signal(
            barrier, inc=1, device_id=coords((me + step) % devices), device_id_type=MESH
        )
        return carry

    lax.fori_loop(1, devices, greet, 0)
    pl.semaphore_wait(barrier, devices - 1)

    mine = pl.ds(my_group * per_old, per_old)
    own_copies = []
    for chunk in range(CHUNKS):
        rows = pl.ds(chunk * piece, piece)
        for step in range(1, groups):
            wanted = (my_group + step) % groups
            remote(
                tables.at[wanted, :, rows, :],
                held[chunk].at[mine],
                grp_send.at[chunk],
                grp_recv.at[chunk],
                (wanted, my_shard),
            ).start()
        own = pltpu.make_async_copy(
            tables.at[my_group, :, rows, :], held[chunk].at[mine], own_grp.at[chunk]
        )
        own.start()
        own_copies.append(own)
        if chunk == 0:
            for step in range(1, groups):
                wanted = (my_group + step) % groups
                remote(
                    sums.at[wanted],
                    held_sums.at[mine],
                    grp_send.at[CHUNKS],
                    grp_recv.at[CHUNKS],
                    (wanted, my_shard),
                ).start()
            own_sums_copy = pltpu.make_async_copy(
                sums.at[my_group], held_sums.at[mine], own_grp.at[CHUNKS]
            )
            own_sums_copy.start()

    def ask(step, carry):
        peer = (me + step) % devices
        remote(
            asking.at[peer], asked.at[me], ask_sem.at[0], ask_sem.at[1], coords(peer)
        ).start()
        return carry

    lax.fori_loop(1, devices, ask, 0)
    own_ask = pltpu.make_async_copy(asking.at[me], asked.at[me], own_sem.at[0])
    own_ask.start()

    order = sorted(range(1, shards), key=lambda step: abs(step - shards // 2))
    others = pl.ds(0, (groups - 1) * per_old)
    other_slots = pl.ds(0, (shards - 1) * capacity)
    own_dev_copies = []

    def exchange(send_ref, got_ref, index):
        for step in order:
            peer = (my_shard + step) % shards
            remote(
                send_ref.at[pl.ds(peer * capacity, capacity)],
                got_ref.at[pl.ds(my_shard * capacity, capacity)],
                dev_send.at[index],
                dev_recv.at[index],
                (my_group, peer),
            ).start()
        own = pltpu.make_async_copy(
            send_ref.at[pl.ds(my_shard * capacity, capacity)],
            got_ref.at[pl.ds(my_shard * capacity, capacity)],
            own_dev.at[index],
        )
        own.start()
        own_dev_copies.append(own)

    for chunk in range(CHUNKS):
        own_copies[chunk].wait()
        remote(
            held[chunk].at[others],
            held[chunk].at[others],
            grp_send.at[chunk],
            grp_recv.at[chunk],
            (my_group, my_shard),
        ).wait_recv()

        def pack(slot, carry):
            send[chunk][slot] = held[chunk][source_of[slot]]
            return carry

        lax.fori_loop(0, slots, pack, 0)
        exchange(send[chunk], got[chunk], chunk)
        if chunk == 0:
            own_sums_copy.wait()
            remote(
                held_sums.at[others],
                held_sums.at[others],
                grp_send.at[CHUNKS],
                grp_recv.at[CHUNKS],
                (my_group, my_shard),
            ).wait_recv()

            def pack_sums(slot, carry):
                send_sums[slot] = held_sums[source_of[slot]]
                return carry

            lax.fori_loop(0, slots, pack_sums, 0)
            exchange(send_sums, got_sums, CHUNKS)

    own_ask.wait()
    remote(
        asked.at[pl.ds(0, devices - 1)],
        asked.at[pl.ds(0, devices - 1)],
        ask_sem.at[0],
        ask_sem.at[1],
        (my_group, my_shard),
    ).wait_recv()
    to_scalar = pltpu.make_async_copy(asked, asked_scalar, own_sem.at[1])
    to_scalar.start()
    to_scalar.wait()

    def arrived(got_ref, index):
        own_dev_copies[index].wait()
        remote(
            got_ref.at[other_slots],
            got_ref.at[other_slots],
            dev_send.at[index],
            dev_recv.at[index],
            (my_group, my_shard),
        ).wait_recv()

    own_dev_copies[:] = [own_dev_copies[0]] + own_dev_copies[2:] + [own_dev_copies[1]]

    arrived(got_sums, CHUNKS)

    def place_sums(place, carry):
        new_sums[place] = got_sums[picker[place]]
        return carry

    lax.fori_loop(0, local, place_sums, 0)

    for chunk in range(CHUNKS):
        arrived(got[chunk], chunk)

        def place_rows(place, carry):
            start = pl.multiple_of(place * tile_rows + chunk * piece, piece)
            table[pl.ds(start, piece), :] = got[chunk][picker[place]]
            return carry

        lax.fori_loop(0, local, place_rows, 0)

    out = pltpu.make_async_copy(table, new_table, out_sem)
    out.start()

    def gather(peer):
        for at in range(limit):
            row = asked_scalar[peer, 0, at]
            answer[peer, at : at + 1, :] = table[pl.ds(row, 1), :]

    def reply(step, carry):
        peer = (me + devices // 2 + step) % devices

        @pl.when(peer != me)
        def _():
            gather(peer)
            remote(
                answer.at[peer], returned.at[me], ans_sem.at[0], ans_sem.at[1], coords(peer)
            ).start()

        return carry

    lax.fori_loop(0, devices, reply, 0)
    gather(me)
    own_answer = pltpu.make_async_copy(answer.at[me], returned.at[me], own_sem.at[2])
    own_answer.start()
    own_answer.wait()
    remote(
        returned.at[pl.ds(0, devices - 1)],
        returned.at[pl.ds(0, devices - 1)],
        ans_sem.at[0],
        ans_sem.at[1],
        (my_group, my_shard),
    ).wait_recv()

    batch = 16

    def look(step, carry):
        for at in range(batch):
            index = final[step * batch + at]
            looked[pl.ds(step * batch + at, 1), :] = returned[
                index // limit, pl.ds(index % limit, 1), :
            ]
        return carry

    lax.fori_loop(0, looked.shape[0] // batch, look, 0)

    for chunk in range(CHUNKS):
        remote(
            held[chunk].at[others],
            held[chunk].at[others],
            grp_send.at[chunk],
            grp_recv.at[chunk],
            (my_group, my_shard),
        ).wait_send()
        remote(
            send[chunk].at[other_slots],
            send[chunk].at[other_slots],
            dev_send.at[chunk],
            dev_recv.at[chunk],
            (my_group, my_shard),
        ).wait_send()
    remote(
        held_sums.at[others],
        held_sums.at[others],
        grp_send.at[CHUNKS],
        grp_recv.at[CHUNKS],
        (my_group, my_shard),
    ).wait_send()
    remote(
        send_sums.at[other_slots],
        send_sums.at[other_slots],
        dev_send.at[CHUNKS],
        dev_recv.at[CHUNKS],
        (my_group, my_shard),
    ).wait_send()
    for ref, sem in ((asked, ask_sem), (returned, ans_sem)):
        remote(
            ref.at[pl.ds(0, devices - 1)],
            ref.at[pl.ds(0, devices - 1)],
            sem.at[0],
            sem.at[1],
            (my_group, my_shard),
        ).wait_send()
    out.wait()


def body(tables, accum, block_position, lookup_ids):
    groups = lax.axis_size("grp")
    shards = lax.axis_size("dev")
    my_group = lax.axis_index("grp")
    my_shard = lax.axis_index("dev")
    table_count, old_rows, width = tables.shape
    per_old = old_rows // TILE
    local = groups * per_old
    longer = local // 2 + 1
    capacity = -(-longer // shards) + -(-(local - longer) // shards)
    look_rows = lookup_ids.shape[0]
    limit = 2 * look_rows // shards
    devices = groups * shards
    i32 = jnp.int32

    position_row = lax.dynamic_index_in_dim(block_position, my_group, 0, keepdims=False)
    by_source = position_row.reshape(groups, shards, per_old)
    places = lax.dynamic_index_in_dim(by_source, my_shard, 1, keepdims=False).reshape(-1)
    target = places // local
    counter = jnp.arange(local, dtype=i32)
    before = (target[:, None] == target[None, :]) & (counter[:, None] < counter[None, :])
    slot_of = target * capacity + jnp.sum(before.astype(i32), axis=0)
    slot = jnp.arange(shards * capacity, dtype=i32)
    source_of = jnp.sum(jnp.where(slot_of[:, None] == slot[None, :], counter[:, None], 0), axis=0)

    old = jnp.arange(position_row.shape[0], dtype=i32)
    place = my_shard * local + counter
    inverse = jnp.sum(jnp.where(position_row[None, :] == place[:, None], old[None, :], 0), axis=1)
    source = inverse // per_old % shards
    rank = inverse // (per_old * shards) * per_old + inverse % per_old
    ahead = (source[:, None] == source[None, :]) & (rank[:, None] < rank[None, :])
    picker = source * capacity + jnp.sum(ahead.astype(i32), axis=0)

    ids = lookup_ids.T
    block_of = ids // TILE
    id_place = jnp.sum(
        jnp.where(block_of[:, None, :] == old[None, :, None], block_position[:, :, None], 0), axis=1
    )
    owner = id_place // local
    local_row = id_place % local * TILE + ids % TILE
    at = jnp.arange(look_rows, dtype=i32)
    earlier = (owner[:, :, None] == owner[:, None, :]) & (at[:, None] < at[None, :])[None]
    seat = owner * limit + jnp.sum(earlier.astype(i32), axis=1)
    seats = jnp.arange(shards * limit, dtype=i32)
    asking = jnp.sum(
        jnp.where(seat[:, :, None] == seats[None, None, :], local_row[:, :, None], 0), axis=1
    )
    asking = asking.reshape(devices, 1, limit)
    lanes = -(-limit // 128) * 128
    asking = jnp.pad(asking, ((0, 0), (0, 0), (0, lanes - limit)))
    final = (jnp.arange(table_count, dtype=i32)[:, None] * (shards * limit) + seat).T.reshape(-1)

    piece = TILE // CHUNKS
    f32 = jnp.float32
    vmem = pl.BlockSpec(memory_space=pltpu.VMEM)
    smem = pl.BlockSpec(memory_space=pltpu.SMEM)
    hbm = pl.BlockSpec(memory_space=pl.ANY)
    new_table, new_sums, looked = pl.pallas_call(
        functools.partial(kernel, groups, shards, capacity, limit),
        out_shape=(
            jax.ShapeDtypeStruct((local * TILE, width), f32),
            jax.ShapeDtypeStruct((local, 1, TILE), f32),
            jax.ShapeDtypeStruct((look_rows * table_count, width), f32),
        ),
        in_specs=[smem, smem, smem, hbm, vmem, vmem],
        out_specs=(hbm, vmem, vmem),
        scratch_shapes=[pltpu.VMEM((local, piece, width), f32) for _ in range(CHUNKS)]
        + [pltpu.VMEM((shards * capacity, piece, width), f32) for _ in range(2 * CHUNKS)]
        + [
            pltpu.VMEM((local, 1, TILE), f32),
            pltpu.VMEM((shards * capacity, 1, TILE), f32),
            pltpu.VMEM((shards * capacity, 1, TILE), f32),
            pltpu.VMEM((local * TILE, width), f32),
            pltpu.VMEM((devices, 1, lanes), i32),
            pltpu.SMEM((devices, 1, lanes), i32),
            pltpu.VMEM((devices, limit, width), f32),
            pltpu.VMEM((devices, limit, width), f32),
            pltpu.SemaphoreType.DMA((CHUNKS + 1,)),
            pltpu.SemaphoreType.DMA((CHUNKS + 1,)),
            pltpu.SemaphoreType.DMA((CHUNKS + 1,)),
            pltpu.SemaphoreType.DMA((CHUNKS + 1,)),
            pltpu.SemaphoreType.DMA((2,)),
            pltpu.SemaphoreType.DMA((2,)),
            pltpu.SemaphoreType.DMA((CHUNKS + 1,)),
            pltpu.SemaphoreType.DMA((CHUNKS + 1,)),
            pltpu.SemaphoreType.DMA((3,)),
            pltpu.SemaphoreType.DMA,
        ],
        compiler_params=pltpu.CompilerParams(
            collective_id=0, has_side_effects=True, vmem_limit_bytes=60 * 1024 * 1024
        ),
    )(
        source_of,
        picker,
        final,
        tables.reshape(table_count, per_old, TILE, width),
        accum.reshape(table_count, per_old, 1, TILE),
        asking,
    )
    return (
        new_table.reshape(1, local * TILE, width),
        new_sums.reshape(1, local * TILE),
        looked.reshape(look_rows, table_count, width),
    )


def solution(mesh):
    placed = (P(None, ("grp", "dev"), None), P(None, ("grp", "dev")), P(), P(("grp", "dev"), None))
    return jax.shard_map(
        body,
        mesh=mesh,
        in_specs=placed,
        out_specs=(P("grp", "dev", None), P("grp", "dev"), P(("grp", "dev"), None, None)),
        check_vma=False,
    )
```

time: 283 us -> 168 us (0.59)
  waiting for transfers between devices: 160 us -> 0 us
  Pallas kernels: 0 us -> 150 us
  local copies, waits for them, and re-layouts: 71.8 us -> 11 us
  starting transfers between devices: 39.1 us -> 0 us
  other arithmetic: 10.6 us -> 4.9 us
    pallas_call x0 -> x1, Pallas kernels: none -> 150 us  [body(): pl.pallas_call(functools.partial(kernel, groups, shards, capacity, limit)...]
    all_to_all x7 -> x0, waiting for transfers between devices: 149 us -> none  [the longest x1 100 us: body(): lax.all_to_all(send_blocks, 'dev', split_axis=0, concat_axis=0, tiled=True)]
    gather x14 -> x0, local copies, waits for them, and re-layouts: 46.7 us -> none  [the longest x1 13.2 us: body(): looked = returned[table_grid, owner, owner_order]]
    all_to_all x7 -> x0, starting transfers between devices: 31.2 us -> none  [the longest x1 6.65 us: body(): lax.all_to_all(send_place, 'dev', split_axis=0, concat_axis=0, tiled=True)]
    ppermute x6 -> x0, waiting for transfers between devices: 10.9 us -> none  [shifted(): lax.ppermute(shard, axis, [(i, (i + by) % peers) for i in range(peers)])]
    ppermute x6 -> x0, starting transfers between devices: 7.92 us -> none  [shifted(): lax.ppermute(shard, axis, [(i, (i + by) % peers) for i in range(peers)])]
    dynamic_update_slice x7 -> x0, local copies, waits for them, and re-layouts: 7.21 us -> none  [the longest x3 6.79 us: body(): held = lax.dynamic_update_index_in_dim(held, got_rows, anchor, 0)]
    mul x2 -> x1, other arithmetic: 5.55 us -> 0.01 us  [body(): jnp.arange(table_count, dtype=i32)[:, None] * (shards * limit) + seat]
  transfers between devices with their start and end apart: 13 -> 0, of which waited for: 7 -> 0; matrix products, arithmetic and copies ran while one was open for 17% -> 0% of each run, Pallas kernels for 0% -> 0%
where the time goes in v1:
time: 168 us; the launch traced here: 166 us
  Pallas kernels  150 us (89%)
  local copies, waits for them, and re-layouts  11 us (7%)
  other arithmetic  4.9 us (3%)
    pallas_call x1, Pallas kernels, body(): pl.pallas_call(functools.partial(kernel, groups, shards, capacity, limit)...  150 us
    unnamed x7, local copies, waits for them, and re-layouts  5.95 us

profile of v1, /device:TPU:0, one launch (start us, length us, event | category | flops | bytes accessed | tf_op | source)
XLA Modules:
  0.0 166.4 jit_solution(17106870700887119549)
XLA Ops:
  0.7 0.5 broadcast.452
  1.2 1.4 fusion.14
  2.5 0.2 select_reduce_fusion.2
  2.7 0.7 add_select_fusion.4
  3.4 1.1 select_reduce_fusion.1
  4.6 0.7 fusion.6
  5.3 0.1 reshape.274
  5.4 0.1 reshape.275
  5.5 0.1 convert_reduce_fusion.1
  5.6 0.5 multiply_add_fusion.1.refs_1_
  6.1 0.1 convert_reduce_fusion.2
  6.2 0.7 select_reduce_fusion.3.refs_0_
  6.9 1.4 reshape.278.refs_4_
  8.3 0.2 convert_reduce_fusion
  8.6 0.1 fusion.4
  8.6 0.4 select_reduce_fusion
  9.1 0.1 reshape.279
  9.2 0.6 pad.4.refs_5_
  9.8 0.1 copy.8
  9.9 0.7 reshape.276.refs_2_
  10.6 149.8 %shard_map.67 = (f32[8192,128]{1,0:T(8,128)}, f32[64,1,128]{2,1,0:T(1,128)}, f32[1024,128]{1,0:T(8,128)}) custom-call(s32[72]{0:T(128)} %select_reduce_fusion.3.refs_0_, s32[64]{0:T(128)} %multiply_add_fusion.1.refs_1_, s32[1024]{0:T(1024)} %reshape.276.refs_2_, f32[4,16,128,128]{3,2,1,0:T(8,128)} %bitcast.45, f32[4,16,1,128]{3,2,1,0:T(1,128)} %reshape.278.refs_4_, ...), custom_call_target="tpu_custom_call" | custom-call | tf_op jit(solution)/shard_map/pallas_call | solution.py:359
  160.4 0.0 copy-start.1
  160.4 0.0 copy-start
  160.5 4.5 %copy.12 = f32[1,8192,128]{2,1,0:T(8,128)} copy(f32[1,8192,128]{2,1,0:T(8,128)} %bitcast.46) | data formatting | bytes 8388608
  165.0 0.0 copy-done.1
  165.0 0.6 copy.13
  165.6 0.0 copy-done
  165.6 0.8 copy.14
  (7 shorter events, 0.1 us)
Async XLA Ops:
  160.4 4.6 %copy-start.1 = (f32[64,1,128]{2,1,0:T(1,128)S(1)}, f32[64,1,128]{2,1,0:T(1,128)}, u32[]{:S(2)}) copy-start(f32[64,1,128]{2,1,0:T(1,128)} %get-tuple-element.7) | copy-start | bytes 98308
  160.4 5.2 %copy-start = (f32[1024,128]{1,0:T(8,128)S(1)}, f32[1024,128]{1,0:T(8,128)}, u32[]{:S(2)}) copy-start(f32[1024,128]{1,0:T(8,128)} %get-tuple-element.8) | copy-start | bytes 1572868

commit v2 on v1

--- a/solution.py
+++ b/solution.py
@@ -8,21 +8,41 @@
 from jax.sharding import PartitionSpec as P
 
 TILE = 128
-CHUNKS = 4
+CHUNKS = 8
+LANES = 128
+SPAN = 512
 MESH = pl.DeviceIdType.MESH
 
 
+def iota(shape, axis):
+    return lax.broadcasted_iota(jnp.int32, shape, axis)
+
+
+def as_row(column, lanes):
+    shape = (column.shape[0], lanes)
+    return jnp.sum(
+        jnp.where(iota(shape, 0) == iota(shape, 1), column, 0), axis=0, keepdims=True
+    )
+
+
 def kernel(groups, shards, capacity, limit, *refs):
-    source_of, picker, final, tables, sums, asking = refs[:6]
-    new_table, new_sums, looked = refs[6:9]
-    held = refs[9 : 9 + CHUNKS]
-    send = refs[9 + CHUNKS : 9 + 2 * CHUNKS]
-    got = refs[9 + 2 * CHUNKS : 9 + 3 * CHUNKS]
+    positions, ids, tables, accum = refs[:4]
+    table, new_sums, looked = refs[4:7]
+    held = refs[7 : 7 + CHUNKS]
+    send = refs[7 + CHUNKS : 7 + 2 * CHUNKS]
+    got = refs[7 + 2 * CHUNKS : 7 + 3 * CHUNKS]
     (
         held_sums,
         send_sums,
         got_sums,
-        table,
+        sums,
+        source_words,
+        picker_words,
+        final_words,
+        source_of,
+        picker,
+        final,
+        asking,
         asked,
         asked_scalar,
         answer,
@@ -36,8 +56,8 @@
         own_grp,
         own_dev,
         own_sem,
-        out_sem,
-    ) = refs[9 + 3 * CHUNKS :]
+        word_sem,
+    ) = refs[7 + 3 * CHUNKS :]
     my_group = lax.axis_index("grp")
     my_shard = lax.axis_index("dev")
     devices = groups * shards
@@ -47,6 +67,71 @@
     piece = tile_rows // CHUNKS
     local = groups * per_old
     slots = shards * capacity
+    table_count, block_count = positions.shape
+    look_rows = ids.shape[0]
+
+    def prepare_source():
+        number = iota((local, 1), 0)
+        place = jnp.zeros((local, 1), jnp.int32)
+        for base in range(0, block_count, SPAN):
+            span = min(SPAN, block_count - base)
+            old = base + iota((local, span), 1)
+            counter = old // (per_old * shards) * per_old + old % per_old
+            match = (old // per_old % shards == my_shard) & (counter == number)
+            row = positions[pl.ds(my_group, 1), base : base + span]
+            place += jnp.sum(jnp.where(match, row, 0), axis=1, keepdims=True)
+        target = place // local
+        lane, line = iota((local, local), 1), iota((local, local), 0)
+        before = (target == as_row(target, local)) & (lane < line)
+        slot_of = target * capacity + jnp.sum(jnp.where(before, 1, 0), axis=1, keepdims=True)
+        slot = iota((local, source_words.shape[1]), 1)
+        source_words[...] = jnp.sum(jnp.where(slot_of == slot, number, 0), axis=0, keepdims=True)
+        copy = pltpu.make_async_copy(source_words, source_of, word_sem.at[0])
+        copy.start()
+        copy.wait()
+
+    def prepare_picker():
+        place = my_shard * local + iota((local, 1), 0)
+        inverse = jnp.zeros((local, 1), jnp.int32)
+        for base in range(0, block_count, SPAN):
+            span = min(SPAN, block_count - base)
+            old = base + iota((local, span), 1)
+            row = positions[pl.ds(my_group, 1), base : base + span]
+            inverse += jnp.sum(jnp.where(row == place, old, 0), axis=1, keepdims=True)
+        source = inverse // per_old % shards
+        rank = inverse // (per_old * shards) * per_old + inverse % per_old
+        ahead = (as_row(source, local) == source) & (as_row(rank, local) < rank)
+        pick = source * capacity + jnp.sum(jnp.where(ahead, 1, 0), axis=1, keepdims=True)
+        picker_words[...] = as_row(pick, picker_words.shape[1])
+        copy = pltpu.make_async_copy(picker_words, picker, word_sem.at[1])
+        copy.start()
+        copy.wait()
+
+    def prepare_requests(index):
+        wanted = ids[:, index : index + 1]
+        block = wanted // tile_rows
+        place = jnp.zeros((look_rows, 1), jnp.int32)
+        for base in range(0, block_count, SPAN):
+            span = min(SPAN, block_count - base)
+            row = positions[index : index + 1, base : base + span]
+            match = block == base + iota((look_rows, span), 1)
+            place += jnp.sum(jnp.where(match, row, 0), axis=1, keepdims=True)
+        owner = place // local
+        local_row = place % local * tile_rows + wanted % tile_rows
+        lane, line = iota((look_rows, look_rows), 1), iota((look_rows, look_rows), 0)
+        before = (owner == as_row(owner, look_rows)) & (lane < line)
+        turn = jnp.sum(jnp.where(before, 1, 0), axis=1, keepdims=True)
+        seat = (index * shards + owner) * limit + turn
+        final_words[index : index + 1, :] = as_row(seat, look_rows)
+
+        def list_rows(shard, carry):
+            match = (owner == shard) & (turn == iota((look_rows, asking.shape[2]), 1))
+            asking[index * shards + shard] = jnp.sum(
+                jnp.where(match, local_row, 0), axis=0, keepdims=True
+            )
+            return carry
+
+        lax.fori_loop(0, shards, list_rows, 0)
 
     def coords(peer):
         return (peer // shards, peer % shards)
@@ -60,6 +145,10 @@
             device_id=device,
             device_id_type=MESH,
         )
+
+    for index in range(table_count):
+        for block in range(per_old):
+            sums[index, block] = accum[index : index + 1, block * tile_rows : (block + 1) * tile_rows]
 
     barrier = pltpu.get_barrier_semaphore()
 
@@ -105,17 +194,6 @@
             )
             own_sums_copy.start()
 
-    def ask(step, carry):
-        peer = (me + step) % devices
-        remote(
-            asking.at[peer], asked.at[me], ask_sem.at[0], ask_sem.at[1], coords(peer)
-        ).start()
-        return carry
-
-    lax.fori_loop(1, devices, ask, 0)
-    own_ask = pltpu.make_async_copy(asking.at[me], asked.at[me], own_sem.at[0])
-    own_ask.start()
-
     order = sorted(range(1, shards), key=lambda step: abs(step - shards // 2))
     others = pl.ds(0, (groups - 1) * per_old)
     other_slots = pl.ds(0, (shards - 1) * capacity)
@@ -139,6 +217,20 @@
         own.start()
         own_dev_copies.append(own)
 
+    def send_requests():
+        def ask(step, carry):
+            peer = (me + step) % devices
+            remote(
+                asking.at[peer], asked.at[me], ask_sem.at[0], ask_sem.at[1], coords(peer)
+            ).start()
+            return carry
+
+        lax.fori_loop(1, devices, ask, 0)
+        own_ask = pltpu.make_async_copy(asking.at[me], asked.at[me], own_sem.at[0])
+        own_ask.start()
+        return own_ask
+
+    prepare_source()
     for chunk in range(CHUNKS):
         own_copies[chunk].wait()
         remote(
@@ -150,7 +242,7 @@
         ).wait_recv()
 
         def pack(slot, carry):
-            send[chunk][slot] = held[chunk][source_of[slot]]
+            send[chunk][slot] = held[chunk][source_of[0, slot]]
             return carry
 
         lax.fori_loop(0, slots, pack, 0)
@@ -166,11 +258,22 @@
             ).wait_recv()
 
             def pack_sums(slot, carry):
-                send_sums[slot] = held_sums[source_of[slot]]
+                send_sums[slot] = held_sums[source_of[0, slot]]
                 return carry
 
             lax.fori_loop(0, slots, pack_sums, 0)
             exchange(send_sums, got_sums, CHUNKS)
+        if chunk < table_count:
+            prepare_requests(chunk)
+        if chunk == min(table_count, CHUNKS) - 1:
+            for index in range(chunk + 1, table_count):
+                prepare_requests(index)
+            own_ask = send_requests()
+
+    prepare_picker()
+    final_copy = pltpu.make_async_copy(final_words, final, word_sem.at[2])
+    final_copy.start()
+    final_copy.wait()
 
     own_ask.wait()
     remote(
@@ -199,7 +302,7 @@
     arrived(got_sums, CHUNKS)
 
     def place_sums(place, carry):
-        new_sums[place] = got_sums[picker[place]]
+        new_sums[place] = got_sums[picker[0, place]]
         return carry
 
     lax.fori_loop(0, local, place_sums, 0)
@@ -209,13 +312,10 @@
 
         def place_rows(place, carry):
             start = pl.multiple_of(place * tile_rows + chunk * piece, piece)
-            table[pl.ds(start, piece), :] = got[chunk][picker[place]]
+            table[pl.ds(start, piece), :] = got[chunk][picker[0, place]]
             return carry
 
         lax.fori_loop(0, local, place_rows, 0)
-
-    out = pltpu.make_async_copy(table, new_table, out_sem)
-    out.start()
 
     def gather(peer):
         for at in range(limit):
@@ -223,41 +323,48 @@
             answer[peer, at : at + 1, :] = table[pl.ds(row, 1), :]
 
     def reply(step, carry):
-        peer = (me + devices // 2 + step) % devices
-
-        @pl.when(peer != me)
-        def _():
-            gather(peer)
-            remote(
-                answer.at[peer], returned.at[me], ans_sem.at[0], ans_sem.at[1], coords(peer)
-            ).start()
-
+        turn = step // groups
+        sign = turn % 2
+        away = shards // 2 + sign * (turn + 1) // 2 - (1 - sign) * (turn // 2)
+        group = (my_group + groups - 1 - step % groups) % groups
+        shard = (my_shard + away) % shards
+        peer = group * shards + shard
+        gather(peer)
+        remote(
+            answer.at[peer],
+            returned.at[pl.ds(me * limit, limit)],
+            ans_sem.at[0],
+            ans_sem.at[1],
+            (group, shard),
+        ).start()
         return carry
 
-    lax.fori_loop(0, devices, reply, 0)
+    lax.fori_loop(0, devices - 1, reply, 0)
     gather(me)
-    own_answer = pltpu.make_async_copy(answer.at[me], returned.at[me], own_sem.at[2])
+    own_answer = pltpu.make_async_copy(
+        answer.at[me], returned.at[pl.ds(me * limit, limit)], own_sem.at[2]
+    )
     own_answer.start()
     own_answer.wait()
     remote(
-        returned.at[pl.ds(0, devices - 1)],
-        returned.at[pl.ds(0, devices - 1)],
+        returned.at[pl.ds(0, (devices - 1) * limit)],
+        returned.at[pl.ds(0, (devices - 1) * limit)],
         ans_sem.at[0],
         ans_sem.at[1],
         (my_group, my_shard),
     ).wait_recv()
 
-    batch = 16
+    batch = 16 // table_count
 
     def look(step, carry):
         for at in range(batch):
-            index = final[step * batch + at]
-            looked[pl.ds(step * batch + at, 1), :] = returned[
-                index // limit, pl.ds(index % limit, 1), :
-            ]
+            for index in range(table_count):
+                line = (step * batch + at) * table_count + index
+                seat = final[index, step * batch + at]
+                looked[pl.ds(line, 1), :] = returned[pl.ds(seat, 1), :]
         return carry
 
-    lax.fori_loop(0, looked.shape[0] // batch, look, 0)
+    lax.fori_loop(0, look_rows // batch, look, 0)
 
     for chunk in range(CHUNKS):
         remote(
@@ -288,22 +395,19 @@
         dev_recv.at[CHUNKS],
         (my_group, my_shard),
     ).wait_send()
-    for ref, sem in ((asked, ask_sem), (returned, ans_sem)):
-        remote(
-            ref.at[pl.ds(0, devices - 1)],
-            ref.at[pl.ds(0, devices - 1)],
+    for ref, sem, count in ((asked, ask_sem, 1), (returned, ans_sem, limit)):
+        remote(
+            ref.at[pl.ds(0, (devices - 1) * count)],
+            ref.at[pl.ds(0, (devices - 1) * count)],
             sem.at[0],
             sem.at[1],
             (my_group, my_shard),
         ).wait_send()
-    out.wait()
 
 
 def body(tables, accum, block_position, lookup_ids):
     groups = lax.axis_size("grp")
     shards = lax.axis_size("dev")
-    my_group = lax.axis_index("grp")
-    my_shard = lax.axis_index("dev")
     table_count, old_rows, width = tables.shape
     per_old = old_rows // TILE
     local = groups * per_old
@@ -313,48 +417,12 @@
     limit = 2 * look_rows // shards
     devices = groups * shards
     i32 = jnp.int32
-
-    position_row = lax.dynamic_index_in_dim(block_position, my_group, 0, keepdims=False)
-    by_source = position_row.reshape(groups, shards, per_old)
-    places = lax.dynamic_index_in_dim(by_source, my_shard, 1, keepdims=False).reshape(-1)
-    target = places // local
-    counter = jnp.arange(local, dtype=i32)
-    before = (target[:, None] == target[None, :]) & (counter[:, None] < counter[None, :])
-    slot_of = target * capacity + jnp.sum(before.astype(i32), axis=0)
-    slot = jnp.arange(shards * capacity, dtype=i32)
-    source_of = jnp.sum(jnp.where(slot_of[:, None] == slot[None, :], counter[:, None], 0), axis=0)
-
-    old = jnp.arange(position_row.shape[0], dtype=i32)
-    place = my_shard * local + counter
-    inverse = jnp.sum(jnp.where(position_row[None, :] == place[:, None], old[None, :], 0), axis=1)
-    source = inverse // per_old % shards
-    rank = inverse // (per_old * shards) * per_old + inverse % per_old
-    ahead = (source[:, None] == source[None, :]) & (rank[:, None] < rank[None, :])
-    picker = source * capacity + jnp.sum(ahead.astype(i32), axis=0)
-
-    ids = lookup_ids.T
-    block_of = ids // TILE
-    id_place = jnp.sum(
-        jnp.where(block_of[:, None, :] == old[None, :, None], block_position[:, :, None], 0), axis=1
-    )
-    owner = id_place // local
-    local_row = id_place % local * TILE + ids % TILE
-    at = jnp.arange(look_rows, dtype=i32)
-    earlier = (owner[:, :, None] == owner[:, None, :]) & (at[:, None] < at[None, :])[None]
-    seat = owner * limit + jnp.sum(earlier.astype(i32), axis=1)
-    seats = jnp.arange(shards * limit, dtype=i32)
-    asking = jnp.sum(
-        jnp.where(seat[:, :, None] == seats[None, None, :], local_row[:, :, None], 0), axis=1
-    )
-    asking = asking.reshape(devices, 1, limit)
-    lanes = -(-limit // 128) * 128
-    asking = jnp.pad(asking, ((0, 0), (0, 0), (0, lanes - limit)))
-    final = (jnp.arange(table_count, dtype=i32)[:, None] * (shards * limit) + seat).T.reshape(-1)
-
+    lanes = -(-limit // LANES) * LANES
+    words = -(-shards * capacity // LANES) * LANES
+    local_lanes = -(-local // LANES) * LANES
     piece = TILE // CHUNKS
     f32 = jnp.float32
     vmem = pl.BlockSpec(memory_space=pltpu.VMEM)
-    smem = pl.BlockSpec(memory_space=pltpu.SMEM)
     hbm = pl.BlockSpec(memory_space=pl.ANY)
     new_table, new_sums, looked = pl.pallas_call(
         functools.partial(kernel, groups, shards, capacity, limit),
@@ -363,19 +431,26 @@
             jax.ShapeDtypeStruct((local, 1, TILE), f32),
             jax.ShapeDtypeStruct((look_rows * table_count, width), f32),
         ),
-        in_specs=[smem, smem, smem, hbm, vmem, vmem],
-        out_specs=(hbm, vmem, vmem),
+        in_specs=[vmem, vmem, hbm, vmem],
+        out_specs=(vmem, vmem, vmem),
         scratch_shapes=[pltpu.VMEM((local, piece, width), f32) for _ in range(CHUNKS)]
         + [pltpu.VMEM((shards * capacity, piece, width), f32) for _ in range(2 * CHUNKS)]
         + [
             pltpu.VMEM((local, 1, TILE), f32),
             pltpu.VMEM((shards * capacity, 1, TILE), f32),
             pltpu.VMEM((shards * capacity, 1, TILE), f32),
-            pltpu.VMEM((local * TILE, width), f32),
+            pltpu.VMEM((table_count, per_old, 1, TILE), f32),
+            pltpu.VMEM((1, words), i32),
+            pltpu.VMEM((1, local_lanes), i32),
+            pltpu.VMEM((table_count, look_rows), i32),
+            pltpu.SMEM((1, words), i32),
+            pltpu.SMEM((1, local_lanes), i32),
+            pltpu.SMEM((table_count, look_rows), i32),
+            pltpu.VMEM((devices, 1, lanes), i32),
             pltpu.VMEM((devices, 1, lanes), i32),
             pltpu.SMEM((devices, 1, lanes), i32),
             pltpu.VMEM((devices, limit, width), f32),
-            pltpu.VMEM((devices, limit, width), f32),
+            pltpu.VMEM((devices * limit, width), f32),
             pltpu.SemaphoreType.DMA((CHUNKS + 1,)),
             pltpu.SemaphoreType.DMA((CHUNKS + 1,)),
             pltpu.SemaphoreType.DMA((CHUNKS + 1,)),
@@ -385,18 +460,16 @@
             pltpu.SemaphoreType.DMA((CHUNKS + 1,)),
             pltpu.SemaphoreType.DMA((CHUNKS + 1,)),
             pltpu.SemaphoreType.DMA((3,)),
-            pltpu.SemaphoreType.DMA,
+            pltpu.SemaphoreType.DMA((3,)),
         ],
         compiler_params=pltpu.CompilerParams(
             collective_id=0, has_side_effects=True, vmem_limit_bytes=60 * 1024 * 1024
         ),
     )(
-        source_of,
-        picker,
-        final,
+        block_position,
+        lookup_ids,
         tables.reshape(table_count, per_old, TILE, width),
-        accum.reshape(table_count, per_old, 1, TILE),
-        asking,
+        accum,
     )
     return (
         new_table.reshape(1, local * TILE, width),

time: 168 us -> 152 us (0.905); the launches traced: 166 us -> 152 us
  Pallas kernels: 150 us -> 144 us
  other arithmetic: 4.9 us -> 0 us
  local copies, waits for them, and re-layouts: 11 us -> 7.43 us
    pallas_call x1, Pallas kernels: 150 us -> 144 us  [body(): pl.pallas_call(functools.partial(kernel, groups, shards, capacity, limit)...]
    reduce_sum x7 -> x0, other arithmetic: 2.84 us -> none  [the longest x1 1.14 us: body(): jnp.sum(jnp.where(block_of[:, None, :] == old[None, :, None], block_posit...]
    reshape x5 -> x0, local copies, waits for them, and re-layouts: 2.39 us -> none  [the longest x1 1.42 us: body(): accum.reshape(table_count, per_old, 1, TILE)]
    dynamic_slice x3 -> x0, local copies, waits for them, and re-layouts: 1.9 us -> none  [the longest x2 1.88 us: body(): lax.dynamic_index_in_dim(block_position, my_group, 0, keepdims=False)]
    unnamed x7 -> x8, local copies, waits for them, and re-layouts: 5.95 us -> 7.43 us
where the time goes in v2:
time: 152 us
  Pallas kernels  144 us (95%)
  local copies, waits for them, and re-layouts  7.43 us (5%)
    pallas_call x1, Pallas kernels, body(): pl.pallas_call(functools.partial(kernel, groups, shards, capacity, limit)...  144 us
    unnamed x8, local copies, waits for them, and re-layouts  7.43 us

profile of v2, /device:TPU:0, one launch (start us, length us, event | category | flops | bytes accessed | tf_op | source)
XLA Modules:
  0.0 152.1 jit_solution(16096939894383229471)
XLA Ops:
  0.6 1.5 copy.7.refs_1_
  2.1 144.0 %shard_map.67 = (f32[8192,128]{1,0:T(8,128)}, f32[64,1,128]{2,1,0:T(1,128)}, f32[1024,128]{1,0:T(8,128)}) custom-call(s32[4,512]{1,0:T(4,128)} %refs_0_.1, s32[256,4]{1,0:T(8,128)} %copy.7.refs_1_, f32[4,16,128,128]{3,2,1,0:T(8,128)} %bitcast.4, f32[4,2048]{1,0:T(4,128)} %refs_3_.1), custom_call_target="tpu_custom_call" | custom-call | tf_op jit(solution)/shard_map/pallas_call | solution.py:427
  146.1 0.0 copy-start.1
  146.1 0.0 copy-start
  146.2 4.5 %copy.11 = f32[1,8192,128]{2,1,0:T(8,128)} copy(f32[1,8192,128]{2,1,0:T(8,128)} %bitcast.5) | data formatting | bytes 8388608
  150.7 0.0 copy-done.1
  150.7 0.6 copy.12
  151.3 0.0 copy-done
  151.3 0.8 copy.13
Async XLA Ops:
  146.1 4.6 %copy-start.1 = (f32[64,1,128]{2,1,0:T(1,128)S(1)}, f32[64,1,128]{2,1,0:T(1,128)}, u32[]{:S(2)}) copy-start(f32[64,1,128]{2,1,0:T(1,128)} %get-tuple-element.7) | copy-start | bytes 98308
  146.1 5.2 %copy-start = (f32[1024,128]{1,0:T(8,128)S(1)}, f32[1024,128]{1,0:T(8,128)}, u32[]{:S(2)}) copy-start(f32[1024,128]{1,0:T(8,128)} %get-tuple-element.8) | copy-start | bytes 1572868

commit v3 on v2

--- a/solution.py
+++ b/solution.py
@@ -8,9 +8,12 @@
 from jax.sharding import PartitionSpec as P
 
 TILE = 128
-CHUNKS = 8
+PIECES = (8, 8, 16, 16, 16, 16, 16, 16, 16)
+STARTS = tuple(sum(PIECES[:index]) for index in range(len(PIECES)))
+CHUNKS = len(PIECES)
 LANES = 128
 SPAN = 512
+UNROLL = 8
 MESH = pl.DeviceIdType.MESH
 
 
@@ -25,8 +28,13 @@
     )
 
 
+def as_column(row):
+    shape = (row.shape[1], row.shape[1])
+    return jnp.sum(jnp.where(iota(shape, 0) == iota(shape, 1), row, 0), axis=1, keepdims=True)
+
+
 def kernel(groups, shards, capacity, limit, *refs):
-    positions, ids, tables, accum = refs[:4]
+    positions_hbm, ids_hbm, tables, accum_hbm = refs[:4]
     table, new_sums, looked = refs[4:7]
     held = refs[7 : 7 + CHUNKS]
     send = refs[7 + CHUNKS : 7 + 2 * CHUNKS]
@@ -35,6 +43,9 @@
         held_sums,
         send_sums,
         got_sums,
+        positions,
+        ids,
+        accum,
         sums,
         source_words,
         picker_words,
@@ -57,6 +68,7 @@
         own_dev,
         own_sem,
         word_sem,
+        load_sem,
     ) = refs[7 + 3 * CHUNKS :]
     my_group = lax.axis_index("grp")
     my_shard = lax.axis_index("dev")
@@ -64,11 +76,10 @@
     me = my_group * shards + my_shard
     per_old = tables.shape[1]
     tile_rows = tables.shape[2]
-    piece = tile_rows // CHUNKS
     local = groups * per_old
     slots = shards * capacity
     table_count, block_count = positions.shape
-    look_rows = ids.shape[0]
+    look_rows = ids.shape[1]
 
     def prepare_source():
         number = iota((local, 1), 0)
@@ -108,7 +119,7 @@
         copy.wait()
 
     def prepare_requests(index):
-        wanted = ids[:, index : index + 1]
+        wanted = as_column(ids[index : index + 1, :])
         block = wanted // tile_rows
         place = jnp.zeros((look_rows, 1), jnp.int32)
         for base in range(0, block_count, SPAN):
@@ -146,9 +157,13 @@
             device_id_type=MESH,
         )
 
-    for index in range(table_count):
-        for block in range(per_old):
-            sums[index, block] = accum[index : index + 1, block * tile_rows : (block + 1) * tile_rows]
+    loads = []
+    for index, (source, target) in enumerate(
+        ((positions_hbm, positions), (ids_hbm, ids), (accum_hbm, accum))
+    ):
+        load = pltpu.make_async_copy(source, target, load_sem.at[index])
+        load.start()
+        loads.append(load)
 
     barrier = pltpu.get_barrier_semaphore()
 
@@ -159,12 +174,18 @@
         return carry
 
     lax.fori_loop(1, devices, greet, 0)
+    for load in loads:
+        load.wait()
+    for index in range(table_count):
+        for block in range(per_old):
+            sums[index, block] = accum[index : index + 1, block * tile_rows : (block + 1) * tile_rows]
+    prepare_source()
     pl.semaphore_wait(barrier, devices - 1)
 
     mine = pl.ds(my_group * per_old, per_old)
     own_copies = []
     for chunk in range(CHUNKS):
-        rows = pl.ds(chunk * piece, piece)
+        rows = pl.ds(STARTS[chunk], PIECES[chunk])
         for step in range(1, groups):
             wanted = (my_group + step) % groups
             remote(
@@ -230,7 +251,6 @@
         own_ask.start()
         return own_ask
 
-    prepare_source()
     for chunk in range(CHUNKS):
         own_copies[chunk].wait()
         remote(
@@ -245,7 +265,7 @@
             send[chunk][slot] = held[chunk][source_of[0, slot]]
             return carry
 
-        lax.fori_loop(0, slots, pack, 0)
+        lax.fori_loop(0, slots, pack, 0, unroll=UNROLL)
         exchange(send[chunk], got[chunk], chunk)
         if chunk == 0:
             own_sums_copy.wait()
@@ -311,11 +331,11 @@
         arrived(got[chunk], chunk)
 
         def place_rows(place, carry):
-            start = pl.multiple_of(place * tile_rows + chunk * piece, piece)
-            table[pl.ds(start, piece), :] = got[chunk][picker[0, place]]
+            start = pl.multiple_of(place * tile_rows + STARTS[chunk], 8)
+            table[pl.ds(start, PIECES[chunk]), :] = got[chunk][picker[0, place]]
             return carry
 
-        lax.fori_loop(0, local, place_rows, 0)
+        lax.fori_loop(0, local, place_rows, 0, unroll=UNROLL)
 
     def gather(peer):
         for at in range(limit):
@@ -420,10 +440,9 @@
     lanes = -(-limit // LANES) * LANES
     words = -(-shards * capacity // LANES) * LANES
     local_lanes = -(-local // LANES) * LANES
-    piece = TILE // CHUNKS
     f32 = jnp.float32
     vmem = pl.BlockSpec(memory_space=pltpu.VMEM)
-    hbm = pl.BlockSpec(memory_space=pl.ANY)
+    hbm = pl.BlockSpec(memory_space=pltpu.HBM)
     new_table, new_sums, looked = pl.pallas_call(
         functools.partial(kernel, groups, shards, capacity, limit),
         out_shape=(
@@ -431,14 +450,17 @@
             jax.ShapeDtypeStruct((local, 1, TILE), f32),
             jax.ShapeDtypeStruct((look_rows * table_count, width), f32),
         ),
-        in_specs=[vmem, vmem, hbm, vmem],
+        in_specs=[hbm, hbm, hbm, hbm],
         out_specs=(vmem, vmem, vmem),
-        scratch_shapes=[pltpu.VMEM((local, piece, width), f32) for _ in range(CHUNKS)]
-        + [pltpu.VMEM((shards * capacity, piece, width), f32) for _ in range(2 * CHUNKS)]
+        scratch_shapes=[pltpu.VMEM((local, piece, width), f32) for piece in PIECES]
+        + [pltpu.VMEM((shards * capacity, piece, width), f32) for piece in PIECES + PIECES]
         + [
             pltpu.VMEM((local, 1, TILE), f32),
             pltpu.VMEM((shards * capacity, 1, TILE), f32),
             pltpu.VMEM((shards * capacity, 1, TILE), f32),
+            pltpu.VMEM(block_position.shape, i32),
+            pltpu.VMEM((table_count, look_rows), i32),
+            pltpu.VMEM(accum.shape, f32),
             pltpu.VMEM((table_count, per_old, 1, TILE), f32),
             pltpu.VMEM((1, words), i32),
             pltpu.VMEM((1, local_lanes), i32),
@@ -461,13 +483,14 @@
             pltpu.SemaphoreType.DMA((CHUNKS + 1,)),
             pltpu.SemaphoreType.DMA((3,)),
             pltpu.SemaphoreType.DMA((3,)),
+            pltpu.SemaphoreType.DMA((3,)),
         ],
         compiler_params=pltpu.CompilerParams(
-            collective_id=0, has_side_effects=True, vmem_limit_bytes=60 * 1024 * 1024
+            collective_id=0, has_side_effects=True, vmem_limit_bytes=32 * 1024 * 1024
         ),
     )(
         block_position,
-        lookup_ids,
+        lookup_ids.T,
         tables.reshape(table_count, per_old, TILE, width),
         accum,
     )

time: 152 us -> 148 us (0.974)
  Pallas kernels: 144 us -> 139 us
    pallas_call x1, Pallas kernels: 144 us -> 139 us  [body(): pl.pallas_call(functools.partial(kernel, groups, shards, capacity, limit)...]
    unnamed x8 -> x11, local copies, waits for them, and re-layouts: 7.43 us -> 7.74 us
where the time goes in v3:
time: 148 us; the launch traced here: 147 us
  Pallas kernels  139 us (94%)
  local copies, waits for them, and re-layouts  7.74 us (5%)
    pallas_call x1, Pallas kernels, body(): pl.pallas_call(functools.partial(kernel, groups, shards, capacity, limit)...  139 us
    unnamed x11, local copies, waits for them, and re-layouts  7.74 us

profile of v3, /device:TPU:0, one launch (start us, length us, event | category | flops | bytes accessed | tf_op | source)
XLA Modules:
  0.0 147.3 jit_solution(11790227400340958008)
XLA Ops:
  0.6 0.0 copy-start
  0.6 2.2 %copy-done = f32[4,2048,128]{2,1,0:T(8,128)S(1)} copy-done((f32[4,2048,128]{2,1,0:T(8,128)S(1)}, f32[4,2048,128]{2,1,0:T(8,128)}, u32[]{:S(2)}) %copy-start) | copy-done | bytes 4194328
  2.8 0.0 copy-start.1
  2.8 0.8 copy-done.1
  3.6 0.0 copy-start.2
  3.6 0.7 copy-done.2
  4.3 0.0 copy-start.3
  4.3 0.7 copy-done.3
  5.0 138.9 %shard_map.67 = (f32[8192,128]{1,0:T(8,128)S(1)}, f32[64,1,128]{2,1,0:T(1,128)S(1)}, f32[1024,128]{1,0:T(8,128)S(1)}) custom-call(s32[4,512]{1,0:T(4,128)S(1)} %copy-done.2, s32[4,256]{1,0:T(4,128)S(1)} %bitcast.9, f32[4,16,128,128]{3,2,1,0:T(8,128)S(1)} %bitcast.5, f32[4,2048]{1,0:T(4,128)S(1)} %copy-done.1), custom_call_target="tpu_custom_call" | custom-call | tf_op jit(solution)/shard_map/pallas_call | solution.py:446
  143.9 2.0 %copy.10 = f32[1,8192,128]{2,1,0:T(8,128)} copy(f32[1,8192,128]{2,1,0:T(8,128)S(1)} %bitcast.6) | data formatting | bytes 8388608
  145.9 0.6 copy.11
  146.5 0.8 copy.12
Async XLA Ops:
  0.6 2.2 %copy-start = (f32[4,2048,128]{2,1,0:T(8,128)S(1)}, f32[4,2048,128]{2,1,0:T(8,128)}, u32[]{:S(2)}) copy-start(f32[4,2048,128]{2,1,0:T(8,128)} %param.4) | copy-start | bytes 12582916
  2.8 0.8 copy-start.1
  3.6 0.7 copy-start.2
  4.3 0.7 copy-start.3
